TPU v7x, 256 devices: a whole 4x4x8 slice. The times are simulated.
256 devices in a mesh: dom: 16 (over y, z_hi, core), orb: 16 (over z_lo, x).
Axes of the slice: x: 4, y: 4, z: 8 (z_hi: 2, z_lo: 4; z = z_hi * 4 + z_lo), core: 2. Of those that a mesh axis runs over, the one named last changes fastest.
Arguments:
- psi: float32 [49152, 2048], P('dom', 'orb'), may hold values from -6 to 6
- rot: float32 [2048, 2048], P(None, 'orb'), may hold values from -0.125 to 0.125
- occ: float32 [2048], P('orb'), may hold values from 0.1 to 2
- v_loc: float32 [49152], P('dom'), may hold values from -1 to 1
Outputs:
- rotated: float32 [49152, 2048], P('dom', 'orb')
- density: float32 [49152], P('dom')
- hpsi: float32 [49152, 2048], P('dom', 'orb')
- band: float32 [2048], P('orb')
All inputs are finite; a program needn't handle non-finite values.
Results may differ from a plain program's by a relative error of at most 0.000075.
Values sent between devices are 32-bit elements; how exact they have to be, the bound alone decides.
A program may use at most 128 MiB of HBM per device.

v0:
```python
import jax
import jax.numpy as jnp
from jax import lax
from jax.sharding import PartitionSpec as P

M = 2048
PLANES_DEV = 3
NY = 8
NZ = 128


def with_halo(cells, sides, width):
    for axis, dim in sides:
        count = lax.axis_size(axis)
        head = lax.slice_in_dim(cells, 0, width, axis=dim)
        tail = lax.slice_in_dim(cells, cells.shape[dim] - width, cells.shape[dim], axis=dim)
        cells = jnp.concatenate(
            [
                lax.ppermute(tail, axis, [(i, (i + 1) % count) for i in range(count)]),
                cells,
                lax.ppermute(head, axis, [((i + 1) % count, i) for i in range(count)]),
            ],
            axis=dim,
        )
    return cells


def shards(psi, rot, occ, v_loc):
    points = psi.shape[0]
    local_m = psi.shape[1]
    rotated = jnp.dot(
        lax.all_gather(psi, "orb", axis=1, tiled=True),
        rot,
        precision=lax.Precision.HIGHEST,
        preferred_element_type=jnp.float32,
    )
    factor = (3.0 / jnp.pi) ** (1.0 / 3.0)
    part_density = jnp.sum(occ[None, :] * rotated * rotated, axis=1) / M
    density = lax.psum(part_density, "orb")
    potential = v_loc - factor * jnp.cbrt(density)
    field = rotated.reshape(PLANES_DEV, NY, NZ, local_m)
    padded = with_halo(field, (("dom", 0),), 1)
    beside = padded[2:] + padded[:-2]
    beside = beside + jnp.roll(field, 1, 1) + jnp.roll(field, -1, 1)
    beside = beside + jnp.roll(field, 1, 2) + jnp.roll(field, -1, 2)
    lap = (beside - 6.0 * field).reshape(points, local_m)
    hpsi = -0.5 * lap + potential[:, None] * rotated
    total_points = points * lax.axis_size("dom")
    band = lax.psum(jnp.sum(rotated * hpsi, axis=0) / total_points, "dom")
    return (rotated, density, hpsi, band)


def solution(mesh):
    placed = (P("dom", "orb"), P(None, "orb"), P("orb"), P("dom"))
    return jax.shard_map(
        shards,
        mesh=mesh,
        in_specs=placed,
        out_specs=(P("dom", "orb"), P("dom"), P("dom", "orb"), P("orb")),
        check_vma=False,
    )
```

profile of v0, /device:TPU:32, one launch (start us, length us, event | category | flops | bytes accessed | tf_op | source)
XLA Modules:
  0.0 473.9 jit_solution(15447638817102200703)
XLA Ops:
  7.2 0.0 copy-start
  7.2 0.0 copy-start.5
  7.2 0.0 all-gather.2.cloned.1.call-start
  7.2 0.7 all-gather.2.cloned.1.call-update
  7.9 279.5 %all-gather.2.cloned.1.call-done = f32[3072,2048]{1,0:T(8,128)} async-done(((f32[3072,128]{1,0:T(8,128)}), f32[3072,2048]{1,0:T(8,128)}) %all-gather.2.cloned.1.call-update) | async-done | bytes 25165840 | tf_op jit(solution)/shard_map/all_gather | solution.py:32
  287.4 0.0 copy-done
  287.4 23.2 %fusion = (f32[3072]{0:T(1024)S(1)}, f32[3072,128]{1,0:T(8,128)S(1)}) fusion(f32[128]{0:T(128)S(1)} %copy-done.5, f32[3072,2048]{1,0:T(8,128)} %all-gather.2.cloned.1.call-done, f32[2048,128]{1,0:T(8,128)S(1)} %copy-done), kind=kOutput, calls=%fused_computation.1 | convolution fusion | flops 9664852992 | bytes 27800064 | tf_op jit(solution)/shard_map/dot_general | solution.py:31
  310.7 0.0 copy-start.1
  310.7 0.7 fusion.9
  311.4 0.9 fusion.12
  312.3 1.9 fusion.10
  314.1 0.6 broadcast_multiply_fusion
  314.7 72.6 %psum.14 = f32[3072]{0:T(1024)} all-reduce(f32[3072]{0:T(1024)} %broadcast_multiply_fusion), channel_id=1, replica_groups=mesh['dom'=16,'orb'=16] {'orb'}, use_global_device_ids=true, to_apply=%region_1.0 | all-reduce | flops 3072 | bytes 24576 | tf_op jit(solution)/shard_map/psum | solution.py:39
  387.3 0.0 collective-permute-start.1
  387.3 7.8 %collective-permute-start = (f32[1,8,128,128]{3,2,1,0:T(8,128)S(1)}, f32[1,8,128,128]{3,2,1,0:T(8,128)S(1)}, u32[]{:S(2)}, u32[]{:S(2)}) collective-permute-start(f32[1,8,128,128]{3,2,1,0:T(8,128)S(1)} %bitcast.13), channel_id=1, source_target_pairs={{16,0},{32,16},{48,32},{64,48},{80,64},{96,80},{112,96},{128,112},... | collective-permute-start | bytes 1572872 | tf_op jit(solution)/shard_map/ppermute | solution.py:21
  395.1 0.7 multiply_subtract_fusion
  395.8 0.0 copy-start.2
  395.9 0.3 fusion.8
  396.2 22.8 %collective-permute-done.1 = f32[1,8,128,128]{3,2,1,0:T(8,128)S(1)} collective-permute-done((f32[1,8,128,128]{3,2,1,0:T(8,128)}, f32[1,8,128,128]{3,2,1,0:T(8,128)S(1)}, u32[]{:S(2)}, u32[]{:S(2)}) %collective-permute-start.1) | collective-permute-done | bytes 524320 | tf_op jit(solution)/shard_map/ppermute | solution.py:19
  419.0 0.0 collective-permute-done
  419.0 0.0 copy-done.3
  419.0 1.1 fusion.7
  420.1 1.6 multiply_reduce_fusion
  421.7 45.3 %psum.15 = f32[128]{0:T(128)} all-reduce(f32[128]{0:T(128)S(1)} %broadcast_multiply_fusion.1), channel_id=1, replica_groups=mesh['dom'=16,'orb'=16] {'dom'}, use_global_device_ids=true, to_apply=%region_3.4 | all-reduce | flops 128 | bytes 1024 | tf_op jit(solution)/shard_map/psum | solution.py:49
  (8 shorter events, 0.0 us)
Async XLA Ops:
  7.2 280.2 %copy-start = (f32[2048,128]{1,0:T(8,128)S(1)}, f32[2048,128]{1,0:T(8,128)}, u32[]{:S(2)}) copy-start(f32[2048,128]{1,0:T(8,128)} %param.5) | copy-start | bytes 3145732
  7.2 280.2 %copy-start.5 = (f32[128]{0:T(128)S(1)}, f32[128]{0:T(128)}, u32[]{:S(2)}) copy-start(f32[128]{0:T(128)} %param.6) | copy-start | bytes 1540
  7.2 280.2 %all-gather.2.cloned.1.call-start = ((), (), s32[]{:S(2)}) async-start(), calls=%async_computation | async-start | bytes 26738688 | tf_op jit(solution)/shard_map/all_gather | solution.py:32
  310.7 109.4 %copy-start.1 = (f32[3072,128]{1,0:T(8,128)}, f32[3072,128]{1,0:T(8,128)S(1)}, u32[]{:S(2)}) copy-start(f32[3072,128]{1,0:T(8,128)S(1)} %get-tuple-element.17) | copy-start | bytes 4718596
  387.3 31.7 %collective-permute-start.1 = (f32[1,8,128,128]{3,2,1,0:T(8,128)}, f32[1,8,128,128]{3,2,1,0:T(8,128)S(1)}, u32[]{:S(2)}, u32[]{:S(2)}) collective-permute-start(f32[1,8,128,128]{3,2,1,0:T(8,128)} %bitcast.14), channel_id=1, source_target_pairs={{0,16},{16,32},{32,48},{48,64},{64,80},{80,96},{96,112},{112,128},... | collective-permute-start | bytes 1572872 | tf_op jit(solution)/shard_map/ppermute | solution.py:19
  387.3 31.7 %collective-permute-start = (f32[1,8,128,128]{3,2,1,0:T(8,128)S(1)}, f32[1,8,128,128]{3,2,1,0:T(8,128)S(1)}, u32[]{:S(2)}, u32[]{:S(2)}) collective-permute-start(f32[1,8,128,128]{3,2,1,0:T(8,128)S(1)} %bitcast.13), channel_id=1, source_target_pairs={{16,0},{32,16},{48,32},{64,48},{80,64},{96,80},{112,96},{128,112},... | collective-permute-start | bytes 1572872 | tf_op jit(solution)/shard_map/ppermute | solution.py:21
  395.8 23.2 %copy-start.2 = (f32[3,7,128,128]{3,2,1,0:T(8,128)S(1)}, f32[3,7,128,128]{3,2,1,0:T(8,128)}, u32[]{:S(2)}) copy-start(f32[3,7,128,128]{3,2,1,0:T(8,128)} %get-tuple-element.10) | copy-start | bytes 4128772
  395.8 23.2 %copy-start.3 = (f32[3,7,128,128]{3,2,1,0:T(8,128)S(1)}, f32[3,7,128,128]{3,2,1,0:T(8,128)}, u32[]{:S(2)}) copy-start(f32[3,7,128,128]{3,2,1,0:T(8,128)} %get-tuple-element.11) | copy-start | bytes 4128772
  395.9 23.1 %copy-start.4 = (f32[3,8,1,128]{3,2,1,0:T(1,128)S(1)}, f32[3,8,1,128]{3,2,1,0:T(1,128)}, u32[]{:S(2)}) copy-start(f32[3,8,1,128]{3,2,1,0:T(1,128)} %get-tuple-element.9) | copy-start | bytes 36868
Sparse Core Ops, SparseCore 0:
  9.7 277.6 all-gather.1
where the time goes:
time: 474 us
  waiting for transfers between devices  303 us (64%)
  blocking collectives  118 us (25%)
  matrix products  23.2 us (5%)
  between operations  14.1 us (3%)
  starting transfers between devices  7.8 us (2%)
    all_gather x1, waiting for transfers between devices, shards(): lax.all_gather(psi, 'orb', axis=1, tiled=True)  279 us
    psum x1, blocking collectives, shards(): density = lax.psum(part_density, 'orb')  72.6 us
    psum x1, blocking collectives, shards(): band = lax.psum(jnp.sum(rotated * hpsi, axis=0) / total_points, 'dom')  45.3 us
    dot_general x1, matrix products, shards(): jnp.dot(lax.all_gather(psi, 'orb', axis=1, tiled=True), rot, precision=la...  23.2 us
    ppermute x1, waiting for transfers between devices, with_halo(): lax.ppermute(tail, axis, [(i, (i + 1) % count) for i in range(count)])  22.8 us
  transfers between devices with their start and end apart: 3, of which 2 were waited for; matrix products, arithmetic and copies ran while one was open for 0% of the time, Pallas kernels for 0%

commit v1 on v0

--- a/solution.py
+++ b/solution.py
@@ -1,3 +1,4 @@
+import functools
 import jax
 import jax.numpy as jnp
 from jax import lax
@@ -7,6 +8,21 @@
 PLANES_DEV = 3
 NY = 8
 NZ = 128
+
+
+def shape_object(x_local, d_out):
+    return jnp.concatenate(
+        jax.lax.all_to_all(
+            jnp.stack([x_local] * jax.lax.axis_size("orb"), axis=0),
+            "orb",
+            split_axis=0,
+            concat_axis=0,
+        ),
+        axis=d_out,
+    )
+
+
+see_the_roads = functools.partial(shape_object, d_out=1)
 
 
 def with_halo(cells, sides, width):
@@ -29,10 +45,7 @@
     points = psi.shape[0]
     local_m = psi.shape[1]
     rotated = jnp.dot(
-        lax.all_gather(psi, "orb", axis=1, tiled=True),
-        rot,
-        precision=lax.Precision.HIGHEST,
-        preferred_element_type=jnp.float32,
+        see_the_roads(psi), rot, precision=lax.Precision.HIGHEST, preferred_element_type=jnp.float32
     )
     factor = (3.0 / jnp.pi) ** (1.0 / 3.0)
     part_density = jnp.sum(occ[None, :] * rotated * rotated, axis=1) / M

time: 474 us -> 762 us (1.61)
  blocking collectives: 118 us -> 668 us
  waiting for transfers between devices: 303 us -> 22.8 us
  matrix products: 23.2 us -> 40.9 us
  local copies, waits for them, and re-layouts: 3.84 us -> 17.4 us
  between operations: 14.1 us -> 0.73 us
    all_to_all x0 -> x1, blocking collectives: none -> 551 us  [shape_object(): jax.lax.all_to_all(jnp.stack([x_local] * jax.lax.axis_size('orb'), axis=0...]
    all_gather x1 -> x0, waiting for transfers between devices: 279 us -> none  [shards(): lax.all_gather(psi, 'orb', axis=1, tiled=True)]
    dot_general x1, matrix products: 23.2 us -> 40.9 us  [shards(): jnp.dot(see_the_roads(psi), rot, precision=lax.Precision.HIGHEST, preferr...]
    another operation x0 -> x1, local copies, waits for them, and re-layouts: none -> 11.6 us  [shape_object(): jnp.stack([x_local] * jax.lax.axis_size('orb'), axis=0)]
  transfers between devices with their start and end apart: 3 -> 2, of which waited for: 2 -> 1; matrix products, arithmetic and copies ran while one was open for 0% -> 0% of each run, Pallas kernels for 0% -> 0%
where the time goes in v1:
time: 762 us
  blocking collectives  668 us (88%)
  matrix products  40.9 us (5%)
  waiting for transfers between devices  22.8 us (3%)
  local copies, waits for them, and re-layouts  17.4 us (2%)
  starting transfers between devices  7.76 us (1%)
    all_to_all x1, blocking collectives, shape_object(): jax.lax.all_to_all(jnp.stack([x_local] * jax.lax.axis_size('orb'), axis=0...  551 us
    psum x1, blocking collectives, shards(): density = lax.psum(part_density, 'orb')  69.6 us
    psum x1, blocking collectives, shards(): band = lax.psum(jnp.sum(rotated * hpsi, axis=0) / total_points, 'dom')  47.3 us
    dot_general x1, matrix products, shards(): jnp.dot(see_the_roads(psi), rot, precision=lax.Precision.HIGHEST, preferr...  40.9 us
    ppermute x1, waiting for transfers between devices, with_halo(): lax.ppermute(tail, axis, [(i, (i + 1) % count) for i in range(count)])  22.7 us
  transfers between devices with their start and end apart: 2, of which 1 were waited for; matrix products, arithmetic and copies ran while one was open for 0% of the time, Pallas kernels for 0%

profile of v1, /device:TPU:32, one launch (start us, length us, event | category | flops | bytes accessed | tf_op | source)
XLA Modules:
  0.0 762.0 jit_solution(6375569501251871585)
XLA Ops:
  0.6 0.0 copy-start
  0.6 2.0 copy.8
  2.6 11.6 %stack.2 = f32[16,3072,128]{1,2,0:T(8,128)} broadcast(f32[3072,128]{0,1:T(8,128)S(1)} %copy.8), dimensions={1,2} | broadcast | bytes 26738688 | tf_op jit(solution)/shard_map/stack | solution.py:16
  14.3 551.5 %all_to_all.5 = f32[16,3072,128]{1,2,0:T(8,128)S(1)} all-to-all(f32[16,3072,128]{1,2,0:T(8,128)} %stack.2), channel_id=1, replica_groups=mesh['dom'=16,'orb'=16] {'orb'}, dimensions={0} | all-to-all | bytes 50331648 | tf_op jit(solution)/shard_map/all_to_all | solution.py:15
  565.7 0.0 copy-done
  565.7 0.0 copy-done.5
  565.7 40.9 %fusion = (f32[3072]{0:T(1024)S(1)}, f32[3072,128]{1,0:T(8,128)S(1)}) fusion(f32[128]{0:T(128)S(1)} %copy-done.5, f32[3072,2048]{0,1:T(8,128)S(1)} %bitcast.11, f32[2048,128]{1,0:T(8,128)S(1)} %copy-done), kind=kOutput, calls=%fused_computation.1 | convolution fusion | flops 9664852992 | bytes 27800064 | tf_op jit(solution)/shard_map/dot_general | solution.py:47
  606.7 0.0 copy-start.1
  606.7 0.7 fusion.9
  607.4 0.9 fusion.12
  608.3 1.9 fusion.10
  610.1 0.6 broadcast_multiply_fusion
  610.7 69.6 %psum.14 = f32[3072]{0:T(1024)} all-reduce(f32[3072]{0:T(1024)} %broadcast_multiply_fusion), channel_id=1, replica_groups=mesh['dom'=16,'orb'=16] {'orb'}, use_global_device_ids=true, to_apply=%region_1.0 | all-reduce | flops 3072 | bytes 24576 | tf_op jit(solution)/shard_map/psum | solution.py:52
  680.3 0.0 collective-permute-start.1
  680.3 7.8 %collective-permute-start = (f32[1,8,128,128]{3,2,1,0:T(8,128)S(1)}, f32[1,8,128,128]{3,2,1,0:T(8,128)S(1)}, u32[]{:S(2)}, u32[]{:S(2)}) collective-permute-start(f32[1,8,128,128]{3,2,1,0:T(8,128)S(1)} %bitcast.17), channel_id=1, source_target_pairs={{16,0},{32,16},{48,32},{64,48},{80,64},{96,80},{112,96},{128,112},... | collective-permute-start | bytes 1572872 | tf_op jit(solution)/shard_map/ppermute | solution.py:37
  688.1 0.7 multiply_subtract_fusion
  688.8 0.0 copy-start.2
  688.9 0.3 fusion.8
  689.2 22.7 %collective-permute-done.1 = f32[1,8,128,128]{3,2,1,0:T(8,128)S(1)} collective-permute-done((f32[1,8,128,128]{3,2,1,0:T(8,128)}, f32[1,8,128,128]{3,2,1,0:T(8,128)S(1)}, u32[]{:S(2)}, u32[]{:S(2)}) %collective-permute-start.1) | collective-permute-done | bytes 524320 | tf_op jit(solution)/shard_map/ppermute | solution.py:35
  712.0 0.0 collective-permute-done
  712.0 0.0 copy-done.2
  712.0 1.1 fusion.7
  713.1 1.6 multiply_reduce_fusion
  714.7 47.3 %psum.15 = f32[128]{0:T(128)} all-reduce(f32[128]{0:T(128)S(1)} %broadcast_multiply_fusion.1), channel_id=1, replica_groups=mesh['dom'=16,'orb'=16] {'dom'}, use_global_device_ids=true, to_apply=%region_3.4 | all-reduce | flops 128 | bytes 1024 | tf_op jit(solution)/shard_map/psum | solution.py:62
  (8 shorter events, 0.0 us)
Async XLA Ops:
  0.6 565.1 %copy-start = (f32[2048,128]{1,0:T(8,128)S(1)}, f32[2048,128]{1,0:T(8,128)}, u32[]{:S(2)}) copy-start(f32[2048,128]{1,0:T(8,128)} %param.5) | copy-start | bytes 3145732
  14.3 551.5 %copy-start.5 = (f32[128]{0:T(128)S(1)}, f32[128]{0:T(128)}, u32[]{:S(2)}) copy-start(f32[128]{0:T(128)} %param.6) | copy-start | bytes 1540
  606.7 106.4 %copy-start.1 = (f32[3072,128]{1,0:T(8,128)}, f32[3072,128]{1,0:T(8,128)S(1)}, u32[]{:S(2)}) copy-start(f32[3072,128]{1,0:T(8,128)S(1)} %get-tuple-element.17) | copy-start | bytes 4718596
  680.3 31.6 %collective-permute-start.1 = (f32[1,8,128,128]{3,2,1,0:T(8,128)}, f32[1,8,128,128]{3,2,1,0:T(8,128)S(1)}, u32[]{:S(2)}, u32[]{:S(2)}) collective-permute-start(f32[1,8,128,128]{3,2,1,0:T(8,128)} %bitcast.18), channel_id=1, source_target_pairs={{0,16},{16,32},{32,48},{48,64},{64,80},{80,96},{96,112},{112,128},... | collective-permute-start | bytes 1572872 | tf_op jit(solution)/shard_map/ppermute | solution.py:35
  680.3 31.6 %collective-permute-start = (f32[1,8,128,128]{3,2,1,0:T(8,128)S(1)}, f32[1,8,128,128]{3,2,1,0:T(8,128)S(1)}, u32[]{:S(2)}, u32[]{:S(2)}) collective-permute-start(f32[1,8,128,128]{3,2,1,0:T(8,128)S(1)} %bitcast.17), channel_id=1, source_target_pairs={{16,0},{32,16},{48,32},{64,48},{80,64},{96,80},{112,96},{128,112},... | collective-permute-start | bytes 1572872 | tf_op jit(solution)/shard_map/ppermute | solution.py:37
  688.8 23.1 %copy-start.2 = (f32[3,7,128,128]{3,2,1,0:T(8,128)S(1)}, f32[3,7,128,128]{3,2,1,0:T(8,128)}, u32[]{:S(2)}) copy-start(f32[3,7,128,128]{3,2,1,0:T(8,128)} %get-tuple-element.10) | copy-start | bytes 4128772
  688.8 23.1 %copy-start.3 = (f32[3,7,128,128]{3,2,1,0:T(8,128)S(1)}, f32[3,7,128,128]{3,2,1,0:T(8,128)}, u32[]{:S(2)}) copy-start(f32[3,7,128,128]{3,2,1,0:T(8,128)} %get-tuple-element.11) | copy-start | bytes 4128772
  688.9 23.1 %copy-start.4 = (f32[3,8,1,128]{3,2,1,0:T(1,128)S(1)}, f32[3,8,1,128]{3,2,1,0:T(1,128)}, u32[]{:S(2)}) copy-start(f32[3,8,1,128]{3,2,1,0:T(1,128)} %get-tuple-element.9) | copy-start | bytes 36868

commit v2 on v0

--- a/solution.py
+++ b/solution.py
@@ -46,7 +46,9 @@
     lap = (beside - 6.0 * field).reshape(points, local_m)
     hpsi = -0.5 * lap + potential[:, None] * rotated
     total_points = points * lax.axis_size("dom")
-    band = lax.psum(jnp.sum(rotated * hpsi, axis=0) / total_points, "dom")
+    part = jnp.sum(rotated * hpsi, axis=0) / total_points
+    parts = lax.all_gather(part, "dom", axis=0, tiled=False)
+    band = parts.sum(axis=0)
     return (rotated, density, hpsi, band)
 
 

time: 474 us -> 456 us (0.962)
  blocking collectives: 118 us -> 98.9 us
    psum x1 -> x0, blocking collectives: 45.3 us -> none  [shards(): band = lax.psum(jnp.sum(rotated * hpsi, axis=0) / total_points, 'dom')]
    all_gather x0 -> x1, blocking collectives: none -> 26.3 us  [shards(): parts = lax.all_gather(part, 'dom', axis=0, tiled=False)]
where the time goes in v2:
time: 456 us; the launch traced here: 455 us
  waiting for transfers between devices  303 us (66%)
  blocking collectives  98.9 us (22%)
  matrix products  23.2 us (5%)
  between operations  14.1 us (3%)
  starting transfers between devices  7.8 us (2%)
  other arithmetic  4.57 us (1%)
    all_gather x1, waiting for transfers between devices, shards(): lax.all_gather(psi, 'orb', axis=1, tiled=True)  279 us
    psum x1, blocking collectives, shards(): density = lax.psum(part_density, 'orb')  72.6 us
    all_gather x1, blocking collectives, shards(): parts = lax.all_gather(part, 'dom', axis=0, tiled=False)  26.3 us
    dot_general x1, matrix products, shards(): jnp.dot(lax.all_gather(psi, 'orb', axis=1, tiled=True), rot, precision=la...  23.2 us
    ppermute x1, waiting for transfers between devices, with_halo(): lax.ppermute(tail, axis, [(i, (i + 1) % count) for i in range(count)])  22.7 us
  transfers between devices with their start and end apart: 3, of which 2 were waited for; matrix products, arithmetic and copies ran while one was open for 0% of the time, Pallas kernels for 0%

profile of v2, /device:TPU:32, one launch (start us, length us, event | category | flops | bytes accessed | tf_op | source)
XLA Modules:
  0.0 455.3 jit_solution(3751056321663245639)
XLA Ops:
  7.2 0.0 copy-start
  7.2 0.0 copy-start.5
  7.2 0.0 all-gather.4.cloned.1.call-start
  7.2 0.7 all-gather.4.cloned.1.call-update
  7.9 279.5 %all-gather.4.cloned.1.call-done = f32[3072,2048]{1,0:T(8,128)} async-done(((f32[3072,128]{1,0:T(8,128)}), f32[3072,2048]{1,0:T(8,128)}) %all-gather.4.cloned.1.call-update) | async-done | bytes 25165840 | tf_op jit(solution)/shard_map/all_gather | solution.py:32
  287.4 23.2 %fusion = (f32[3072]{0:T(1024)S(1)}, f32[3072,128]{1,0:T(8,128)S(1)}) fusion(f32[128]{0:T(128)S(1)} %copy-done.5, f32[3072,2048]{1,0:T(8,128)} %all-gather.4.cloned.1.call-done, f32[2048,128]{1,0:T(8,128)S(1)} %copy-done), kind=kOutput, calls=%fused_computation.1 | convolution fusion | flops 9664852992 | bytes 27800064 | tf_op jit(solution)/shard_map/dot_general | solution.py:31
  310.7 0.0 copy-start.1
  310.7 0.7 fusion.9
  311.4 0.9 fusion.12
  312.3 1.9 fusion.10
  314.1 0.6 broadcast_multiply_fusion
  314.7 72.6 %psum.7 = f32[3072]{0:T(1024)} all-reduce(f32[3072]{0:T(1024)} %broadcast_multiply_fusion), channel_id=1, replica_groups=mesh['dom'=16,'orb'=16] {'orb'}, use_global_device_ids=true, to_apply=%region_1.0 | all-reduce | flops 3072 | bytes 24576 | tf_op jit(solution)/shard_map/psum | solution.py:39
  387.3 0.0 collective-permute-start.1
  387.3 7.8 %collective-permute-start = (f32[1,8,128,128]{3,2,1,0:T(8,128)S(1)}, f32[1,8,128,128]{3,2,1,0:T(8,128)S(1)}, u32[]{:S(2)}, u32[]{:S(2)}) collective-permute-start(f32[1,8,128,128]{3,2,1,0:T(8,128)S(1)} %bitcast.15), channel_id=1, source_target_pairs={{16,0},{32,16},{48,32},{64,48},{80,64},{96,80},{112,96},{128,112},... | collective-permute-start | bytes 1572872 | tf_op jit(solution)/shard_map/ppermute | solution.py:21
  395.1 0.7 multiply_subtract_fusion
  395.8 0.0 copy-start.2
  395.9 0.3 fusion.8
  396.2 22.7 %collective-permute-done.1 = f32[1,8,128,128]{3,2,1,0:T(8,128)S(1)} collective-permute-done((f32[1,8,128,128]{3,2,1,0:T(8,128)}, f32[1,8,128,128]{3,2,1,0:T(8,128)S(1)}, u32[]{:S(2)}, u32[]{:S(2)}) %collective-permute-start.1) | collective-permute-done | bytes 524320 | tf_op jit(solution)/shard_map/ppermute | solution.py:19
  418.9 0.0 collective-permute-done
  418.9 0.0 copy-done.2
  418.9 1.1 fusion.7
  420.0 1.6 multiply_reduce_fusion
  421.6 26.3 %all-gather.1 = f32[16,1,128]{2,1,0:T(1,128)S(1)} all-gather(f32[1,1,128]{2,1,0:T(1,128)S(1)} %multiply_bitcast_fusion), channel_id=2, replica_groups=mesh['dom'=16,'orb'=16] {'dom'}, dimensions={0}, use_global_device_ids=true | all-gather | bytes 8704 | tf_op jit(solution)/shard_map/all_gather | solution.py:50
  447.9 0.5 reduce_sum.29
  (9 shorter events, 0.0 us)
Async XLA Ops:
  7.2 280.2 %copy-start = (f32[2048,128]{1,0:T(8,128)S(1)}, f32[2048,128]{1,0:T(8,128)}, u32[]{:S(2)}) copy-start(f32[2048,128]{1,0:T(8,128)} %param.5) | copy-start | bytes 3145732
  7.2 280.2 %copy-start.5 = (f32[128]{0:T(128)S(1)}, f32[128]{0:T(128)}, u32[]{:S(2)}) copy-start(f32[128]{0:T(128)} %param.6) | copy-start | bytes 1540
  7.2 280.2 %all-gather.4.cloned.1.call-start = ((), (), s32[]{:S(2)}) async-start(), calls=%async_computation | async-start | bytes 26738688 | tf_op jit(solution)/shard_map/all_gather | solution.py:32
  310.7 109.4 %copy-start.1 = (f32[3072,128]{1,0:T(8,128)}, f32[3072,128]{1,0:T(8,128)S(1)}, u32[]{:S(2)}) copy-start(f32[3072,128]{1,0:T(8,128)S(1)} %get-tuple-element.17) | copy-start | bytes 4718596
  387.3 31.6 %collective-permute-start.1 = (f32[1,8,128,128]{3,2,1,0:T(8,128)}, f32[1,8,128,128]{3,2,1,0:T(8,128)S(1)}, u32[]{:S(2)}, u32[]{:S(2)}) collective-permute-start(f32[1,8,128,128]{3,2,1,0:T(8,128)} %bitcast.16), channel_id=1, source_target_pairs={{0,16},{16,32},{32,48},{48,64},{64,80},{80,96},{96,112},{112,128},... | collective-permute-start | bytes 1572872 | tf_op jit(solution)/shard_map/ppermute | solution.py:19
  387.3 31.6 %collective-permute-start = (f32[1,8,128,128]{3,2,1,0:T(8,128)S(1)}, f32[1,8,128,128]{3,2,1,0:T(8,128)S(1)}, u32[]{:S(2)}, u32[]{:S(2)}) collective-permute-start(f32[1,8,128,128]{3,2,1,0:T(8,128)S(1)} %bitcast.15), channel_id=1, source_target_pairs={{16,0},{32,16},{48,32},{64,48},{80,64},{96,80},{112,96},{128,112},... | collective-permute-start | bytes 1572872 | tf_op jit(solution)/shard_map/ppermute | solution.py:21
  395.8 23.1 %copy-start.2 = (f32[3,7,128,128]{3,2,1,0:T(8,128)S(1)}, f32[3,7,128,128]{3,2,1,0:T(8,128)}, u32[]{:S(2)}) copy-start(f32[3,7,128,128]{3,2,1,0:T(8,128)} %get-tuple-element.10) | copy-start | bytes 4128772
  395.8 23.1 %copy-start.3 = (f32[3,7,128,128]{3,2,1,0:T(8,128)S(1)}, f32[3,7,128,128]{3,2,1,0:T(8,128)}, u32[]{:S(2)}) copy-start(f32[3,7,128,128]{3,2,1,0:T(8,128)} %get-tuple-element.11) | copy-start | bytes 4128772
  395.9 23.1 %copy-start.4 = (f32[3,8,1,128]{3,2,1,0:T(1,128)S(1)}, f32[3,8,1,128]{3,2,1,0:T(1,128)}, u32[]{:S(2)}) copy-start(f32[3,8,1,128]{3,2,1,0:T(1,128)} %get-tuple-element.9) | copy-start | bytes 36868
Sparse Core Ops, SparseCore 0:
  9.7 277.6 all-gather.3
